TPU v7x, 32 devices: a whole 2x2x4 slice. The times are simulated.
32 devices in a mesh: group: 4 (over x, core), member: 8 (over z, y).
Axes of the slice: x: 2, y: 2, z: 4, core: 2. Of those that a mesh axis runs over, the one named last changes fastest.
Arguments:
- queries: bfloat16 [32, 32, 128], P(('group', 'member')), may hold values from -1.2 to 1.2
- pages: bfloat16 [192, 1024, 128], P(('group', 'member')), may hold values from -1.2 to 1.2
- users: int32 [192, 32], P(('group', 'member')), may hold values from 0 to 31, as said below
- page_count: int32 [192], P(('group', 'member')), may hold values from 1 to 32
- teacher: float32 [192, 32], P(('group', 'member')), may hold values from 4 to 12
Outputs:
- scores: float32 [192, 32], P(('group', 'member'))
- query_grad: float32 [32, 32, 128], P(('group', 'member'))
- page_grad: bfloat16 [192, 1024, 128], P(('group', 'member'))
Inputs may be any that keep to these rules, and one draw needn't show every extreme that they name: `users`: slots at or past page_count hold valid ids that are ignored. Queries are numbered in the order of their owning devices. Over the slots of the pages of one device, exactly 8 distinct queries of each group (of 8 consecutive query ids) appear, counting dead slots too.
All inputs are finite; a program needn't handle non-finite values.
Results may differ from a plain program's by a relative error of at most 0.014.
Values may be sent and summed in bfloat16 or wider, within the bound.
No kernel may reach another device: no remote copies, remote signals or barrier semaphores. Data moves between devices by JAX's collectives and lax.ppermute only.
A program may use at most 64 MiB of HBM per device.

v0:
```python
import jax
import jax.numpy as jnp
from jax import lax
from jax.sharding import PartitionSpec as P

CAP = 8


normalized_exponent_divisor = 0.05


def body(queries, pages, users, page_count, teacher):
    gathered = lax.all_gather(queries, ("group", "member"), axis=0, tiled=True)
    slots = users.shape[1]
    tok_rows = queries.shape[1]
    width = queries.shape[2]
    features = tok_rows * width

    def page_step(unused, inputs):
        page_tile, user_row, active_total, teacher_row = inputs
        chosen = gathered[user_row].reshape(slots * tok_rows, width)
        cosine_affinity = lax.dot_general(
            chosen, page_tile, (((1,), (1,)), ((), ())), preferred_element_type=jnp.float32
        )
        pairing_coefficients = jax.nn.softmax(
            cosine_affinity / normalized_exponent_divisor, axis=-1
        )
        aligned_rating = jnp.sum(pairing_coefficients * cosine_affinity, axis=-1)
        score = jnp.sum(aligned_rating.reshape(slots, tok_rows), axis=-1)
        live = lax.iota(jnp.int32, slots) < active_total
        unaligned_rating = jnp.where(live, score - teacher_row, 0.0)
        mismatch_row_set = jnp.repeat(unaligned_rating, tok_rows)
        rating_gradient_factor = (
            mismatch_row_set[:, None]
            * pairing_coefficients
            * (1.0 + (cosine_affinity - aligned_rating[:, None]) / normalized_exponent_divisor)
        ).astype(jnp.bfloat16)
        query_part = jnp.dot(rating_gradient_factor, page_tile, preferred_element_type=jnp.float32)
        page_part = lax.dot_general(
            rating_gradient_factor,
            chosen,
            (((0,), (0,)), ((), ())),
            preferred_element_type=jnp.float32,
        )
        return (
            unused,
            (
                jnp.where(live, score, 0.0),
                query_part.reshape(slots, features),
                page_part.astype(jnp.bfloat16),
            ),
        )

    _, (scores, query_terms, page_grad) = lax.scan(
        page_step, jnp.int32(0), (pages, users, page_count, teacher)
    )
    flat_users = users.reshape(-1)
    stacked = query_terms.reshape(-1, features)
    group_rows = lax.axis_size("member") * queries.shape[0]
    num_groups = lax.axis_size("group")
    query_ids = lax.iota(jnp.int32, num_groups * group_rows)
    slot_match = query_ids[:, None] == flat_users[None, :]
    used = jnp.any(slot_match, axis=1).reshape(num_groups, group_rows)
    rank = jnp.cumsum(used.astype(jnp.int32), axis=1) - 1
    slot_rank = jnp.sum(jnp.where(slot_match, rank.reshape(-1)[:, None], 0), axis=0)
    position = flat_users // group_rows * CAP + slot_rank
    placing = (lax.iota(jnp.int32, num_groups * CAP)[:, None] == position[None, :]).astype(
        jnp.float32
    )
    send_rows = jnp.dot(
        placing, stacked, precision=lax.Precision.HIGHEST, preferred_element_type=jnp.float32
    )
    send_rows = send_rows.reshape(num_groups, CAP, features)
    member_rows = lax.iota(jnp.int32, group_rows)
    hits = used[:, :, None] & (rank[:, :, None] == lax.iota(jnp.int32, CAP)[None, None, :])
    found = jnp.sum(jnp.where(hits, member_rows[None, :, None], 0), axis=1)
    send_ids = jnp.where(jnp.any(hits, axis=1), found, -1).astype(jnp.float32)
    recv_rows, recv_ids = (
        lax.all_to_all(
            send_rows.astype(jnp.bfloat16), "group", split_axis=0, concat_axis=0, tiled=True
        ).astype(send_rows.dtype),
        lax.all_to_all(
            send_ids.astype(jnp.bfloat16), "group", split_axis=0, concat_axis=0, tiled=True
        ).astype(send_ids.dtype),
    )
    landing = (member_rows.astype(jnp.float32)[:, None] == recv_ids.reshape(-1)[None, :]).astype(
        jnp.float32
    )
    table = jnp.dot(
        landing,
        recv_rows.reshape(-1, features),
        precision=lax.Precision.HIGHEST,
        preferred_element_type=jnp.float32,
    )
    own_rows = lax.psum_scatter(
        table.astype(jnp.bfloat16), "member", scatter_dimension=0, tiled=True
    ).astype(jnp.float32)
    query_grad = own_rows.reshape(queries.shape)
    return (scores, query_grad, page_grad)


def solution(mesh):
    placed = (
        P(("group", "member"), None, None),
        P(("group", "member"), None, None),
        P(("group", "member"), None),
        P(("group", "member")),
        P(("group", "member"), None),
    )
    return jax.shard_map(
        body,
        mesh=mesh,
        in_specs=placed,
        out_specs=(
            P(("group", "member"), None),
            P(("group", "member"), None, None),
            P(("group", "member"), None, None),
        ),
        check_vma=False,
    )
```

profile of v0, /device:TPU:0, one launch (start us, length us, event | category | flops | bytes accessed | tf_op | source)
XLA Modules:
  0.0 284.1 jit_solution(4698372575317380719)
XLA Ops:
  9.1 4.2 %all-to-all-start = ((bf16[4,1,8]{2,1,0:T(2,128)(2,1)}), bf16[4,1,8]{2,1,0:T(2,128)(2,1)S(1)}, u32[]{:S(2)}, u32[]{:S(2)}) async-start(bf16[4,1,8]{2,1,0:T(2,128)(2,1)} %copy.9), calls=%async_computation | async-start | bytes 4096 | tf_op jit(solution)/shard_map/all_to_all | solution.py:82
  13.5 76.1 %all_gather.3 = bf16[32,32,128]{2,1,0:T(8,128)(2,1)} all-gather(bf16[1,32,128]{2,1,0:T(8,128)(2,1)} %param.7), channel_id=1, replica_groups=mesh['group'=4,'member'=8] {'group','member'}, dimensions={0}, use_global_device_ids=true | all-gather | bytes 270336 | tf_op jit(solution)/shard_map/all_gather | solution.py:13
  89.6 105.8 %while.14 = (s32[]{:T(128)}, f32[6,32]{1,0:T(8,128)S(1)}, f32[6,32,4096]{2,1,0:T(8,128)}, bf16[6,1024,128]{2,1,0:T(8,128)(2,1)}, s32[6]{0:T(128)}, /*index=5*/s3...) while((s32[]{:T(128)}, f32[6,32]{1,0:T(8,128)S(1)}, ...), condition=%wide.region_5.6_spmd, body=%wide.region_0.5_spmd.sunk | while | flops 825359616 | bytes 44373960 | solution.py:54
  90.3 1.6 gather_fusion
  91.8 1.7 multiply_reduce_fusion.4
  94.3 1.2 copy-done
  98.0 1.4 compare_select_fusion.6
  99.5 3.6 %multiply_convert_fusion.2 = bf16[1024,1024]{0,1:T(8,128)(2,1)S(1)} fusion(f32[1024,1024]{0,1:T(8,128)} %copy-done, f32[1024]{0:T(1024)S(1)} %multiply_reduce_fusion.5, f32[1024]{0:T(1024)S(1)} %mul.39, f32[1024]{0:T(1024)S(1)} %fusion.47, f32[1024]{0:T(1024)S(1)} %get-tuple-element.133), kind=kLoop, calls=%fused_computation.1.clone.1 | loop fusion | flops 9437184 | bytes 6307840 | tf_op jit(solution)/shard_map/while/body/eval_jaxpr/convert_element_type | solution.py:37
  103.1 1.7 fusion.48
  105.8 1.4 fusion.49
  107.9 1.6 gather_fusion
  109.4 1.7 multiply_reduce_fusion.4
  111.9 1.2 copy-done
  115.6 1.4 compare_select_fusion.6
  117.1 3.6 %multiply_convert_fusion.2 = bf16[1024,1024]{0,1:T(8,128)(2,1)S(1)} fusion(f32[1024,1024]{0,1:T(8,128)} %copy-done, f32[1024]{0:T(1024)S(1)} %multiply_reduce_fusion.5, f32[1024]{0:T(1024)S(1)} %mul.39, f32[1024]{0:T(1024)S(1)} %fusion.47, f32[1024]{0:T(1024)S(1)} %get-tuple-element.133), kind=kLoop, calls=%fused_computation.1.clone.1 | loop fusion | flops 9437184 | bytes 6307840 | tf_op jit(solution)/shard_map/while/body/eval_jaxpr/convert_element_type | solution.py:37
  120.7 1.7 fusion.48
  123.4 1.4 fusion.49
  125.5 1.6 gather_fusion
  127.1 1.7 multiply_reduce_fusion.4
  129.5 1.2 copy-done
  133.2 1.4 compare_select_fusion.6
  134.8 3.6 %multiply_convert_fusion.2 = bf16[1024,1024]{0,1:T(8,128)(2,1)S(1)} fusion(f32[1024,1024]{0,1:T(8,128)} %copy-done, f32[1024]{0:T(1024)S(1)} %multiply_reduce_fusion.5, f32[1024]{0:T(1024)S(1)} %mul.39, f32[1024]{0:T(1024)S(1)} %fusion.47, f32[1024]{0:T(1024)S(1)} %get-tuple-element.133), kind=kLoop, calls=%fused_computation.1.clone.1 | loop fusion | flops 9437184 | bytes 6307840 | tf_op jit(solution)/shard_map/while/body/eval_jaxpr/convert_element_type | solution.py:37
  138.4 1.7 fusion.48
  141.0 1.4 fusion.49
  143.2 1.6 gather_fusion
  144.7 1.7 multiply_reduce_fusion.4
  147.2 1.2 copy-done
  150.9 1.4 compare_select_fusion.6
  152.4 3.6 %multiply_convert_fusion.2 = bf16[1024,1024]{0,1:T(8,128)(2,1)S(1)} fusion(f32[1024,1024]{0,1:T(8,128)} %copy-done, f32[1024]{0:T(1024)S(1)} %multiply_reduce_fusion.5, f32[1024]{0:T(1024)S(1)} %mul.39, f32[1024]{0:T(1024)S(1)} %fusion.47, f32[1024]{0:T(1024)S(1)} %get-tuple-element.133), kind=kLoop, calls=%fused_computation.1.clone.1 | loop fusion | flops 9437184 | bytes 6307840 | tf_op jit(solution)/shard_map/while/body/eval_jaxpr/convert_element_type | solution.py:37
  156.0 1.7 fusion.48
  158.7 1.4 fusion.49
  160.8 1.6 gather_fusion
  162.3 1.7 multiply_reduce_fusion.4
  168.5 1.4 compare_select_fusion.6
  170.0 3.6 %multiply_convert_fusion.2 = bf16[1024,1024]{0,1:T(8,128)(2,1)S(1)} fusion(f32[1024,1024]{0,1:T(8,128)} %copy-done, f32[1024]{0:T(1024)S(1)} %multiply_reduce_fusion.5, f32[1024]{0:T(1024)S(1)} %mul.39, f32[1024]{0:T(1024)S(1)} %fusion.47, f32[1024]{0:T(1024)S(1)} %get-tuple-element.133), kind=kLoop, calls=%fused_computation.1.clone.1 | loop fusion | flops 9437184 | bytes 6307840 | tf_op jit(solution)/shard_map/while/body/eval_jaxpr/convert_element_type | solution.py:37
  173.6 1.7 fusion.48
  176.3 1.4 fusion.49
  178.4 1.6 gather_fusion
  180.0 1.7 multiply_reduce_fusion.4
  186.1 1.4 compare_select_fusion.6
  187.7 3.6 %multiply_convert_fusion.2 = bf16[1024,1024]{0,1:T(8,128)(2,1)S(1)} fusion(f32[1024,1024]{0,1:T(8,128)} %copy-done, f32[1024]{0:T(1024)S(1)} %multiply_reduce_fusion.5, f32[1024]{0:T(1024)S(1)} %mul.39, f32[1024]{0:T(1024)S(1)} %fusion.47, f32[1024]{0:T(1024)S(1)} %get-tuple-element.133), kind=kLoop, calls=%fused_computation.1.clone.1 | loop fusion | flops 9437184 | bytes 6307840 | tf_op jit(solution)/shard_map/while/body/eval_jaxpr/convert_element_type | solution.py:37
  191.3 1.7 fusion.48
  194.0 1.4 fusion.49
  195.5 3.9 %convolution_convert_fusion.1 = bf16[4,8,4096]{2,1,0:T(8,128)(2,1)} fusion(f32[192,4096,1]{1,0,2:T(8,128)} %bitcast.72, s32[192]{0:T(256)S(1)} %multiply_add_fusion.1, s32[4,8]{1,0:T(4,128)S(1)} %multiply_add_fusion), kind=kOutput, calls=%fused_computation.29 | convolution fusion | flops 302127104 | bytes 3408768 | tf_op jit(solution)/shard_map/dot_general | solution.py:70
  199.4 3.4 %all-to-all-start.1 = ((bf16[4,8,4096]{2,1,0:T(8,128)(2,1)}), bf16[4,8,4096]{2,1,0:T(8,128)(2,1)S(1)}, u32[]{:S(2)}, u32[]{:S(2)}) async-start(bf16[4,8,4096]{2,1,0:T(8,128)(2,1)} %convolution_convert_fusion.1), calls=%async_computation.1 | async-start | bytes 524288 | tf_op jit(solution)/shard_map/all_to_all | solution.py:79
  203.0 5.8 %all-to-all-done.1 = bf16[4,8,4096]{2,1,0:T(8,128)(2,1)S(1)} async-done(((bf16[4,8,4096]{2,1,0:T(8,128)(2,1)}), bf16[4,8,4096]{2,1,0:T(8,128)(2,1)S(1)}, u32[]{:S(2)}, u32[]{:S(2)}) %all-to-all-start.1) | async-done | bytes 262176 | tf_op jit(solution)/shard_map/all_to_all | solution.py:79
  210.2 65.0 %all-reduce.3.cloned.1.call-done = bf16[8,4096]{1,0:T(8,128)(2,1)} async-done(((bf16[8,4096]{1,0:T(8,128)(2,1)}), bf16[8,4096]{1,0:T(8,128)(2,1)}) %all-reduce.3.cloned.1.call-update) | async-done | bytes 65552
  275.2 2.0 dynamic-slice_convert_fusion
  (127 shorter events, 36.5 us)
Async XLA Ops:
  9.1 190.3 %all-to-all-start = ((bf16[4,1,8]{2,1,0:T(2,128)(2,1)}), bf16[4,1,8]{2,1,0:T(2,128)(2,1)S(1)}, u32[]{:S(2)}, u32[]{:S(2)}) async-start(bf16[4,1,8]{2,1,0:T(2,128)(2,1)} %copy.9), calls=%async_computation | async-start | bytes 4096 | tf_op jit(solution)/shard_map/all_to_all | solution.py:82
  93.5 1.9 copy-start
  93.5 3.1 %copy-start.2 = (s32[6]{0:T(128)S(1)}, s32[6]{0:T(128)}, u32[]{:S(2)}) copy-start(s32[6]{0:T(128)} %get-tuple-element.162) | copy-start | bytes 76 | tf_op jit(solution)/shard_map/while
  111.1 1.9 copy-start
  111.1 3.1 %copy-start.2 = (s32[6]{0:T(128)S(1)}, s32[6]{0:T(128)}, u32[]{:S(2)}) copy-start(s32[6]{0:T(128)} %get-tuple-element.162) | copy-start | bytes 76 | tf_op jit(solution)/shard_map/while
  128.8 1.9 copy-start
  128.8 3.1 %copy-start.2 = (s32[6]{0:T(128)S(1)}, s32[6]{0:T(128)}, u32[]{:S(2)}) copy-start(s32[6]{0:T(128)} %get-tuple-element.162) | copy-start | bytes 76 | tf_op jit(solution)/shard_map/while
  146.4 1.9 copy-start
  146.4 3.1 %copy-start.2 = (s32[6]{0:T(128)S(1)}, s32[6]{0:T(128)}, u32[]{:S(2)}) copy-start(s32[6]{0:T(128)} %get-tuple-element.162) | copy-start | bytes 76 | tf_op jit(solution)/shard_map/while
  164.0 1.9 copy-start
  164.0 3.1 %copy-start.2 = (s32[6]{0:T(128)S(1)}, s32[6]{0:T(128)}, u32[]{:S(2)}) copy-start(s32[6]{0:T(128)} %get-tuple-element.162) | copy-start | bytes 76 | tf_op jit(solution)/shard_map/while
  181.7 1.9 copy-start
  181.7 3.1 %copy-start.2 = (s32[6]{0:T(128)S(1)}, s32[6]{0:T(128)}, u32[]{:S(2)}) copy-start(s32[6]{0:T(128)} %get-tuple-element.162) | copy-start | bytes 76 | tf_op jit(solution)/shard_map/while
  195.4 81.8 %copy-start.1 = (f32[6,32]{1,0:T(8,128)}, f32[6,32]{1,0:T(8,128)S(1)}, u32[]{:S(2)}) copy-start(f32[6,32]{1,0:T(8,128)S(1)} %get-tuple-element.49) | copy-start | bytes 2308
  195.4 14.3 %copy-start.3 = (u32[32]{0:T(128)S(1)}, u32[32]{0:T(128)}, u32[]{:S(2)}) copy-start(u32[32]{0:T(128)} %constant.71) | copy-start | bytes 388
  199.4 9.4 %all-to-all-start.1 = ((bf16[4,8,4096]{2,1,0:T(8,128)(2,1)}), bf16[4,8,4096]{2,1,0:T(8,128)(2,1)S(1)}, u32[]{:S(2)}, u32[]{:S(2)}) async-start(bf16[4,8,4096]{2,1,0:T(8,128)(2,1)} %convolution_convert_fusion.1), calls=%async_computation.1 | async-start | bytes 524288 | tf_op jit(solution)/shard_map/all_to_all | solution.py:79
  202.8 72.4 %all-reduce.3.cloned.1.call-start = ((), (), s32[]{:S(2)}) async-start(), calls=%async_computation.2 | async-start | bytes 131072
Sparse Core Ops, SparseCore 0:
  209.8 65.3 all-reduce.2
where the time goes:
time: 286 us; the launch traced here: 284 us
  blocking collectives  76.1 us (27%)
  waiting for transfers between devices  70.8 us (25%)
  other arithmetic  51.8 us (18%)
  matrix products  33.5 us (12%)
  local copies, waits for them, and re-layouts  29.8 us (10%)
  between operations  14.1 us (5%)
  starting transfers between devices  7.68 us (3%)
    all_gather x1, blocking collectives, body(): gathered = lax.all_gather(queries, ('group', 'member'), axis=0, tiled=True)  76.1 us
    unnamed x2, waiting for transfers between devices  65 us
    convert_element_type x6, other arithmetic, page_step(): rating_gradient_factor = (mismatch_row_set[:, None] * pairing_coefficient...  21.7 us
    dot_general x6, matrix products, page_step(): jnp.dot(rating_gradient_factor, page_tile, preferred_element_type=jnp.flo...  10.2 us
    dot_general x6, matrix products, page_step(): lax.dot_general(chosen, page_tile, (((1,), (1,)), ((), ())), preferred_el...  10 us
    gather x6, local copies, waits for them, and re-layouts, page_step(): chosen = gathered[user_row].reshape(slots * tok_rows, width)  9.31 us
    dot_general x6, matrix products, page_step(): lax.dot_general(rating_gradient_factor, chosen, (((0,), (0,)), ((), ())),...  8.5 us
    select_n x6, other arithmetic, page_step(): unaligned_rating = jnp.where(live, score - teacher_row, 0.0)  8.25 us
  transfers between devices with their start and end apart: 3, of which 2 were waited for; matrix products, arithmetic and copies ran while one was open for 36% of the time, Pallas kernels for 0%

commit v1 on v0

v1 whole, which is shorter than its diff:
```python
import functools

import jax
import jax.numpy as jnp
from jax import lax
from jax.experimental import pallas as pl
from jax.experimental.pallas import tpu as pltpu
from jax.sharding import PartitionSpec as P

AXES = ("group", "member")
BLOCK = 8
INV_TEMP = 20.0
LOG2E = 1.4426950408889634


def grad_kernel(order, blocks, q_ref, page_ref, page_t_ref, cnt_ref, sum_ref, diag_ref,
                dq_ref, slope_ref, score_ref, qb, sim, wts, acc):
    n_pages, p_tok, dim = page_ref.shape
    n_tok = q_ref.shape[1]
    width = BLOCK * n_tok
    per_page = slope_ref.shape[0] // n_pages
    acc[...] = jnp.zeros_like(acc)
    chunk = 64
    parts = [pl.ds(r, chunk) for r in range(0, p_tok, chunk)]

    def fold(x, op):
        x = x.reshape(chunk // 8, 8, width)
        out = x[0]
        for i in range(1, chunk // 8):
            out = op(out, x[i])
        return out

    def block_step(p, j):
        b = p * per_page + j
        for k in range(BLOCK):
            qb[pl.ds(k * n_tok, n_tok), :] = q_ref[order[p, j * BLOCK + k]]
        sim[...] = lax.dot_general(
            page_ref[p], qb[...], (((1,), (1,)), ((), ())), preferred_element_type=jnp.float32
        )
        top = fold(sim[parts[0], :], jnp.maximum)
        for r in parts[1:]:
            top = jnp.maximum(top, fold(sim[r, :], jnp.maximum))
        top = jnp.max(top, axis=0, keepdims=True)
        total = jnp.zeros((8, width), jnp.float32)
        mass = jnp.zeros((8, width), jnp.float32)
        for r in parts:
            s = sim[r, :]
            e = jnp.exp2((s - top) * (INV_TEMP * LOG2E))
            wts[r, :] = e
            total += fold(e, jnp.add)
            mass += fold(e * s, jnp.add)
        inv = 1.0 / jnp.sum(total, axis=0, keepdims=True)
        matched = jnp.sum(mass, axis=0, keepdims=True) * inv
        hi = matched.astype(jnp.bfloat16)
        rest = matched - hi.astype(jnp.float32)
        mid = rest.astype(jnp.bfloat16)
        low = (rest - mid.astype(jnp.float32)).astype(jnp.bfloat16)
        pieces = jnp.concatenate([hi, mid, low], axis=0)
        score = jnp.sum(
            jnp.dot(pieces, diag_ref[...], preferred_element_type=jnp.float32),
            axis=0, keepdims=True)
        score_ref[b] = score
        mismatch = cnt_ref[b] * score - sum_ref[b]
        scale = mismatch * inv
        beta = scale * INV_TEMP
        alpha = scale - beta * matched
        for r in parts:
            slope_ref[b, r, :] = (wts[r, :] * (alpha + beta * sim[r, :])).astype(jnp.bfloat16)
        part_t = jnp.dot(page_t_ref[p], slope_ref[b], preferred_element_type=jnp.float32)
        part = part_t.T
        for k in range(BLOCK):
            acc[order[p, j * BLOCK + k]] += part[k * n_tok:(k + 1) * n_tok, :]

    def page_step(p, carry):
        def inner(j, c):
            block_step(p, j)
            return c
        return lax.fori_loop(0, blocks[p], inner, carry)

    lax.fori_loop(0, n_pages, page_step, 0)
    dq_ref[...] = acc[...].astype(dq_ref.dtype)


def page_kernel(order, blocks, q_ref, slope_ref, out_ref, qb):
    n_pages, p_tok, dim = out_ref.shape
    n_tok = q_ref.shape[1]
    width = BLOCK * n_tok
    per_page = slope_ref.shape[0] // n_pages
    for p in range(n_pages):
        for k in range(per_page * BLOCK):
            qb[pl.ds(k * n_tok, n_tok), :] = q_ref[order[p, k]]
        for n in range(1, per_page + 1):
            @pl.when(blocks[p] == n)
            def _():
                total = jnp.dot(slope_ref[p * per_page], qb[pl.ds(0, width), :],
                                preferred_element_type=jnp.float32)
                for j in range(1, n):
                    total += jnp.dot(slope_ref[p * per_page + j], qb[pl.ds(j * width, width), :],
                                     preferred_element_type=jnp.float32)
                out_ref[p] = total.astype(out_ref.dtype)


def body(queries, pages, users, page_count, teacher):
    n_dev = lax.axis_size("group") * lax.axis_size("member")
    own, n_tok, dim = queries.shape
    n_pages, p_tok, _ = pages.shape
    slots = users.shape[1]
    n_query = n_dev * own
    per_page = slots // BLOCK
    n_blocks = n_pages * per_page
    width = BLOCK * n_tok

    copies = jnp.broadcast_to(queries[None], (n_dev, own, n_tok, dim))
    gathered = lax.all_to_all(copies, AXES, split_axis=0, concat_axis=0, tiled=True)
    gathered = gathered.reshape(n_query, n_tok, dim)

    slot_ids = lax.iota(jnp.int32, slots)
    live = slot_ids[None, :] < page_count[:, None]
    same = (users[:, :, None] == users[:, None, :]) & live[:, :, None] & live[:, None, :]
    earlier = slot_ids[None, :] < slot_ids[:, None]
    first = live & ~jnp.any(same & earlier[None], axis=2)
    rank = jnp.sum(jnp.where(first[:, None, :] & earlier[None], 1, 0), axis=2)
    put = first[:, :, None] & (rank[:, :, None] == slot_ids[None, None, :])
    order = jnp.sum(jnp.where(put, users[:, :, None], 0), axis=1)
    number = jnp.sum(first.astype(jnp.int32), axis=1)
    blocks = (number + BLOCK - 1) // BLOCK
    hits = jnp.sum(same.astype(jnp.float32), axis=2)
    aims = jnp.sum(jnp.where(same, teacher[:, None, :], 0.0), axis=2)
    cnt = jnp.sum(jnp.where(put, hits[:, :, None], 0.0), axis=1)
    aim = jnp.sum(jnp.where(put, aims[:, :, None], 0.0), axis=1)
    place = jnp.sum(jnp.where(same & first[:, None, :], rank[:, None, :], 0), axis=2)

    def lanes(x):
        return jnp.repeat(x.reshape(n_blocks, 1, BLOCK), n_tok, axis=2)

    lane = lax.iota(jnp.int32, width) // n_tok
    diag = (lane[:, None] == lane[None, :]).astype(jnp.bfloat16)
    page_t = jnp.swapaxes(pages, 1, 2)

    smem = pl.BlockSpec(memory_space=pltpu.SMEM)
    vmem = pl.BlockSpec(memory_space=pltpu.VMEM)
    dq, slope, score = pl.pallas_call(
        grad_kernel,
        out_shape=(
            jax.ShapeDtypeStruct((n_query, n_tok, dim), jnp.bfloat16),
            jax.ShapeDtypeStruct((n_blocks, p_tok, width), jnp.bfloat16),
            jax.ShapeDtypeStruct((n_blocks, 1, width), jnp.float32),
        ),
        in_specs=[smem, smem] + [vmem] * 6,
        out_specs=(vmem, vmem, vmem),
        scratch_shapes=[
            pltpu.VMEM((width, dim), jnp.bfloat16),
            pltpu.VMEM((p_tok, width), jnp.float32),
            pltpu.VMEM((p_tok, width), jnp.float32),
            pltpu.VMEM((n_query, n_tok, dim), jnp.float32),
        ],
        compiler_params=pltpu.CompilerParams(vmem_limit_bytes=32 << 20),
        cost_estimate=pl.CostEstimate(flops=4 * 10**9, bytes_accessed=4 << 20, transcendentals=4 << 20),
        name="grad",
    )(order, blocks, gathered, pages, page_t, lanes(cnt), lanes(aim), diag)

    terms = lax.all_to_all(
        dq.reshape(n_dev, own, n_tok, dim), AXES, split_axis=0, concat_axis=0, tiled=True)

    page_grad = pl.pallas_call(
        page_kernel,
        out_shape=jax.ShapeDtypeStruct(pages.shape, pages.dtype),
        in_specs=[smem, smem, vmem, vmem],
        out_specs=vmem,
        scratch_shapes=[pltpu.VMEM((slots * n_tok, dim), jnp.bfloat16)],
        compiler_params=pltpu.CompilerParams(vmem_limit_bytes=32 << 20),
        cost_estimate=pl.CostEstimate(flops=2 * 10**9, bytes_accessed=4 << 20, transcendentals=0),
        name="page_part",
    )(order, blocks, gathered, slope)

    ranked = score.reshape(n_pages, slots, n_tok)[:, :, 0]
    found = place[:, :, None] == slot_ids[None, None, :]
    scores = jnp.sum(jnp.where(found & live[:, :, None], ranked[:, None, :], 0.0), axis=2)
    query_grad = jnp.sum(terms.astype(jnp.float32), axis=0)
    return scores, query_grad, page_grad


def solution(mesh):
    row = P(AXES)
    return jax.shard_map(
        body,
        mesh=mesh,
        in_specs=(P(AXES, None, None), P(AXES, None, None), P(AXES, None), row, P(AXES, None)),
        out_specs=(P(AXES, None), P(AXES, None, None), P(AXES, None, None)),
        check_vma=False,
    )
```

time: 286 us -> 64.5 us (0.23)
  blocking collectives: 76.1 us -> 0 us
  waiting for transfers between devices: 70.8 us -> 0.65 us
  other arithmetic: 51.8 us -> 9.54 us
  matrix products: 33.5 us -> 0 us
  Pallas kernels: 0 us -> 22 us
  local copies, waits for them, and re-layouts: 29.8 us -> 16.1 us
  between operations: 14.1 us -> 0.76 us
  starting transfers between devices: 7.68 us -> 14.1 us
    all_gather x1 -> x0, blocking collectives: 76.1 us -> none  [body(): gathered = lax.all_gather(queries, ('group', 'member'), axis=0, tiled=True)]
    unnamed x2 -> x0, waiting for transfers between devices: 65 us -> none
    dot_general x20 -> x0, matrix products: 33.5 us -> none  [the longest x6 10.2 us: page_step(): jnp.dot(rating_gradient_factor, page_tile, preferred_element_type=jnp.flo...]
    pallas_call x0 -> x2, Pallas kernels: none -> 22 us  [the longest x1 17.4 us: body(): pl.pallas_call(grad_kernel, out_shape=(jax.ShapeDtypeStruct((n_query, n_t...]
    convert_element_type x10 -> x1, other arithmetic: 21.7 us -> 0.1 us  [body(): diag = (lane[:, None] == lane[None, :]).astype(jnp.bfloat16)]
    select_n x18 -> x2, other arithmetic: 16.5 us -> 0.01 us  [the longest x1 0.01 us: body(): blocks = (number + BLOCK - 1) // BLOCK]
    unnamed x5 -> x16, local copies, waits for them, and re-layouts: 0.59 us -> 12.7 us
    gather x6 -> x0, local copies, waits for them, and re-layouts: 9.31 us -> none  [page_step(): chosen = gathered[user_row].reshape(slots * tok_rows, width)]
  transfers between devices with their start and end apart: 3 -> 2, of which waited for: 2 -> 1; matrix products, arithmetic and copies ran while one was open for 36% -> 18% of each run, Pallas kernels for 0% -> 7%
where the time goes in v1:
time: 64.5 us; the launch traced here: 63.2 us
  Pallas kernels  22 us (34%)
  local copies, waits for them, and re-layouts  16.1 us (25%)
  starting transfers between devices  14.1 us (22%)
  other arithmetic  9.54 us (15%)
  between operations  0.76 us (1%)
  waiting for transfers between devices  0.65 us (1%)
    pallas_call x1, Pallas kernels, body(): pl.pallas_call(grad_kernel, out_shape=(jax.ShapeDtypeStruct((n_query, n_t...  17.4 us
    unnamed x16, local copies, waits for them, and re-layouts  12.7 us
    all_to_all x1, starting transfers between devices, body(): lax.all_to_all(copies, AXES, split_axis=0, concat_axis=0, tiled=True)  7.33 us
    all_to_all x1, starting transfers between devices, body(): lax.all_to_all(dq.reshape(n_dev, own, n_tok, dim), AXES, split_axis=0, co...  6.79 us
    pallas_call x1, Pallas kernels, body(): pl.pallas_call(page_kernel, out_shape=jax.ShapeDtypeStruct(pages.shape, p...  4.6 us
    broadcast_in_dim x1, other arithmetic, body(): aim = jnp.sum(jnp.where(put, aims[:, :, None], 0.0), axis=1)  1.64 us
    broadcast_in_dim x1, other arithmetic, body(): cnt = jnp.sum(jnp.where(put, hits[:, :, None], 0.0), axis=1)  1.64 us
    broadcast_in_dim x4, local copies, waits for them, and re-layouts, lanes(): return jnp.repeat(x.reshape(n_blocks, 1, BLOCK), n_tok, axis=2)  1.59 us
  transfers between devices with their start and end apart: 2, of which 1 were waited for; matrix products, arithmetic and copies ran while one was open for 18% of the time, Pallas kernels for 7%

profile of v1, /device:TPU:0, one launch (start us, length us, event | category | flops | bytes accessed | tf_op | source)
XLA Modules:
  0.0 63.2 jit_solution(12646002651234799903)
XLA Ops:
  0.6 0.0 copy-start.2
  0.6 1.6 %broadcast_in_dim.109 = bf16[32,1,32,128]{3,2,1,0:T(8,128)(2,1)} broadcast(bf16[32,128]{1,0:T(8,128)(2,1)} %bitcast.16), dimensions={2,3} | broadcast | bytes 270336 | tf_op jit(solution)/shard_map/broadcast_in_dim | solution.py:113
  2.2 7.3 %all-to-all-start = ((bf16[32,1,32,128]{3,2,1,0:T(8,128)(2,1)}), bf16[32,1,32,128]{3,2,1,0:T(8,128)(2,1)S(1)}, u32[]{:S(2)}, u32[]{:S(2)}) async-start(bf16[32,1,32,128]{3,2,1,0:T(8,128)(2,1)} %broadcast_in_dim.109), calls=%async_computation | async-start | bytes 524288 | tf_op jit(solution)/shard_map/all_to_all | solution.py:114
  9.5 0.7 %iota_compare_fusion.3 = pred[6,32]{1,0:T(8,128)(4,1)S(1)} fusion(s32[6]{0:T(128)} %param.8), kind=kLoop, calls=%fused_computation.24 | loop fusion | flops 192 | bytes 216 | tf_op jit(solution)/shard_map/lt | solution.py:118
  10.3 1.0 %and_reduce_fusion = pred[6,32]{1,0:T(8,128)(4,1)S(1)} fusion(pred[32,32]{1,0:T(8,128)(4,1)S(1)} %iota_compare_fusion.2, pred[6,32]{1,0:T(8,128)(4,1)S(1)} %iota_compare_fusion.3, s32[6,32]{1,0:T(8,128)} %param.7), kind=kLoop, calls=%fused_computation.18 | loop fusion | flops 30528 | bytes 2176 | tf_op jit(solution)/shard_map/reduce_or | solution.py:121
  11.3 0.8 %convert_reduce_fusion.2 = (s32[6]{0:T(128)S(1)}, pred[6,32]{1,0:T(8,128)(4,1)S(1)}) fusion(pred[6,32]{1,0:T(8,128)(4,1)S(1)} %and_reduce_fusion, s32[6]{0:T(128)} %param.8), kind=kLoop, calls=%fused_computation.23 | loop fusion | flops 954 | bytes 432 | tf_op jit(solution)/shard_map/reduce_sum | solution.py:125
  12.2 0.2 select_reduce_fusion.4
  12.4 1.6 %fusion.11 = f32[6,32]{1,0:T(8,128)S(1)} fusion(pred[6,32]{1,0:T(8,128)(4,1)S(1)} %iota_compare_fusion.3, s32[6,32]{1,0:T(8,128)} %param.7, s32[6,32]{1,0:T(8,128)S(1)} %select_reduce_fusion.4, pred[6,32]{1,0:T(8,128)(4,1)S(1)} %get-tuple-element.12), kind=kOutput, calls=%fused_computation.35 | output fusion | flops 49183 | bytes 2688 | tf_op jit(solution)/shard_map/jit(_where)/broadcast_in_dim | solution.py:129
  14.0 1.1 %select_reduce_fusion.3 = (s32[6,32]{1,0:T(8,128)S(1)}, s32[6,32]{1,0:T(8,128)S(1)}) fusion(s32[6,32]{1,0:T(8,128)S(1)} %select_reduce_fusion.4, pred[6,32]{1,0:T(8,128)(4,1)S(1)} %get-tuple-element.12, pred[6,32]{1,0:T(8,128)(4,1)S(1)} %iota_compare_fusion.3, s32[6,32]{1,0:T(8,128)} %param.7), kind=kLoop, calls=%fused_computation.14 | loop fusion | flops 61056 | bytes 3456 | tf_op jit(solution)/shard_map/reduce_sum | solution.py:131
  15.1 1.6 %fusion.12 = f32[6,32]{1,0:T(8,128)S(1)} fusion(f32[6,32]{1,0:T(8,128)} %param.9, pred[6,32]{1,0:T(8,128)(4,1)S(1)} %iota_compare_fusion.3, s32[6,32]{1,0:T(8,128)} %param.7, s32[6,32]{1,0:T(8,128)S(1)} %select_reduce_fusion.4, pred[6,32]{1,0:T(8,128)(4,1)S(1)} %get-tuple-element.12), kind=kOutput, calls=%fused_computation.36 | output fusion | flops 49183 | bytes 3456 | tf_op jit(solution)/shard_map/jit(_where)/broadcast_in_dim | solution.py:130
  16.7 0.1 reshape.160
  16.8 0.1 reshape.159
  16.9 0.1 broadcast_in_dim.112
  17.0 0.7 %broadcast_in_dim.113.cnt_ref = f32[24,1,256]{2,1,0:T(1,128)} reshape(f32[24,8,32]{2,1,0:T(8,128)S(1)} %broadcast_in_dim.112) | data formatting | bytes 49152 | tf_op jit(solution)/shard_map/broadcast_in_dim | solution.py:134
  17.7 0.1 broadcast_in_dim.116
  17.8 0.7 %broadcast_in_dim.117.sum_ref = f32[24,1,256]{2,1,0:T(1,128)} reshape(f32[24,8,32]{2,1,0:T(8,128)S(1)} %broadcast_in_dim.116) | data formatting | bytes 49152 | tf_op jit(solution)/shard_map/broadcast_in_dim | solution.py:134
  18.5 0.0 copy-done.2
  18.5 0.7 %copy.14 = bf16[6,1024,128]{1,2,0:T(8,128)(2,1)S(1)} copy(bf16[6,1024,128]{2,1,0:T(8,128)(2,1)S(1)} %copy-done.2) | data formatting | bytes 3145728 | tf_op args[1]
  19.2 0.1 compare_convert_fusion.diag_ref
  19.3 0.6 %all-to-all-done = bf16[32,1,32,128]{3,2,1,0:T(8,128)(2,1)S(1)} async-done(((bf16[32,1,32,128]{3,2,1,0:T(8,128)(2,1)}), bf16[32,1,32,128]{3,2,1,0:T(8,128)(2,1)S(1)}, u32[]{:S(2)}, u32[]{:S(2)}) %all-to-all-start) | async-done | bytes 262176 | tf_op jit(solution)/shard_map/all_to_all | solution.py:114
  20.0 0.0 copy-start.5
  20.0 0.7 %copy-done.5 = f32[24,1,256]{2,1,0:T(1,128)S(1)} copy-done((f32[24,1,256]{2,1,0:T(1,128)S(1)}, f32[24,1,256]{2,1,0:T(1,128)}, u32[]{:S(2)}) %copy-start.5) | copy-done | bytes 24600
  20.7 0.0 copy-start.6
  20.7 0.7 %copy-done.6 = f32[24,1,256]{2,1,0:T(1,128)S(1)} copy-done((f32[24,1,256]{2,1,0:T(1,128)S(1)}, f32[24,1,256]{2,1,0:T(1,128)}, u32[]{:S(2)}) %copy-start.6) | copy-done | bytes 24600
  21.4 17.4 %grad.1 = (bf16[32,32,128]{2,1,0:T(8,128)(2,1)S(1)}, bf16[24,1024,256]{2,1,0:T(8,128)(2,1)S(1)}, f32[24,1,256]{2,1,0:T(1,128)S(1)}) custom-call(s32[6,32]{1,0:T(8,128)S(1)} %get-tuple-element.10.order, s32[6]{0:T(128)S(1)} %and_select_fusion.1.blocks, bf16[32,32,128]{2,1,0:T(8,128)(2,1)S(1)} %bitcast.10, bf16[6,1024,128]{2,1,0:T(8,128)(2,1)S(1)} %copy-done.2, ...), custom_call_target="tpu_custom_call" | custom-call | flops 4000000000 | bytes 4194304 | tf_op jit(solution)/shard_map/grad/pallas_call | solution.py:142
  38.9 0.0 copy-start
  38.9 4.6 %copy-done = bf16[24,1024,256]{2,1,0:T(8,128)(2,1)} copy-done((bf16[24,1024,256]{2,1,0:T(8,128)(2,1)}, bf16[24,1024,256]{2,1,0:T(8,128)(2,1)S(1)}, u32[]{:S(2)}) %copy-start) | copy-done | bytes 12582936
  43.4 0.0 copy-start.3
  43.5 0.7 %copy-done.3 = bf16[32,32,128]{2,1,0:T(8,128)(2,1)} copy-done((bf16[32,32,128]{2,1,0:T(8,128)(2,1)}, bf16[32,32,128]{2,1,0:T(8,128)(2,1)S(1)}, u32[]{:S(2)}) %copy-start.3) | copy-done | bytes 262168
  44.2 0.0 copy-start.4
  44.2 0.6 copy-done.4
  44.8 6.8 %all-to-all-start.1 = ((bf16[32,1,32,128]{3,2,1,0:T(8,128)(2,1)}), bf16[32,1,32,128]{3,2,1,0:T(8,128)(2,1)S(1)}, u32[]{:S(2)}, u32[]{:S(2)}) async-start(bf16[32,1,32,128]{3,2,1,0:T(8,128)(2,1)} %bitcast.12), calls=%async_computation.1 | async-start | bytes 524288 | tf_op jit(solution)/shard_map/all_to_all | solution.py:162
  51.6 0.8 %reduce.1 = f32[24,256]{1,0:T(8,128)S(1)} reduce(f32[24,1,256]{2,1,0:T(1,128)} %copy-done.4, f32[]{:T(128)} %constant.48), dimensions={1}, to_apply=%get-tuple-element.6.reduce_sub_computation | reduce | bytes 49156 | tf_op jit(solution)/shard_map/grad/pallas_call | solution.py:142
  52.4 0.1 reshape.161
  52.4 0.1 copy.17
  52.6 0.8 %select_reduce_fusion.1 = f32[6,32]{1,0:T(8,128)} fusion(f32[6,32]{1,0:T(8,128)S(1)} %bitcast.15, s32[6,32]{1,0:T(8,128)S(1)} %get-tuple-element.9, pred[6,32]{1,0:T(8,128)(4,1)S(1)} %iota_compare_fusion.3), kind=kLoop, calls=%fused_computation.10 | loop fusion | flops 24384 | bytes 2496 | tf_op jit(solution)/shard_map/reduce_sum | solution.py:178
  53.4 0.0 copy-start.1
  53.4 4.6 %copy-done.1 = bf16[24,1024,256]{2,1,0:T(8,128)(2,1)S(1)} copy-done((bf16[24,1024,256]{2,1,0:T(8,128)(2,1)S(1)}, bf16[24,1024,256]{2,1,0:T(8,128)(2,1)}, u32[]{:S(2)}) %copy-start.1) | copy-done | bytes 12582936
  57.9 4.6 %page_part.1 = bf16[6,1024,128]{2,1,0:T(8,128)(2,1)} custom-call(s32[6,32]{1,0:T(8,128)S(1)} %get-tuple-element.10.order, s32[6]{0:T(128)S(1)} %and_select_fusion.1.blocks, bf16[32,32,128]{2,1,0:T(8,128)(2,1)S(1)} %bitcast.11, bf16[24,1024,256]{2,1,0:T(8,128)(2,1)S(1)} %copy-done.1), custom_call_target="tpu_custom_call" | custom-call | flops 2000000000 | bytes 4194304 | tf_op jit(solution)/shard_map/page_part/pallas_call | solution.py:165
  62.5 0.0 all-to-all-done.1
  62.5 0.7 %convert_reduce_fusion = f32[32,128]{1,0:T(8,128)} fusion(bf16[32,1,32,128]{3,2,1,0:T(8,128)(2,1)S(1)} %all-to-all-done.1), kind=kLoop, calls=%fused_computation.4 | loop fusion | flops 258048 | bytes 278528 | tf_op jit(solution)/shard_map/reduce_sum | solution.py:179
  (3 shorter events, 0.0 us)
Async XLA Ops:
  0.6 17.9 %copy-start.2 = (bf16[6,1024,128]{2,1,0:T(8,128)(2,1)S(1)}, bf16[6,1024,128]{2,1,0:T(8,128)(2,1)}, u32[]{:S(2)}) copy-start(bf16[6,1024,128]{2,1,0:T(8,128)(2,1)} %page_ref.1) | copy-start | bytes 4718596
  2.2 17.8 %all-to-all-start = ((bf16[32,1,32,128]{3,2,1,0:T(8,128)(2,1)}), bf16[32,1,32,128]{3,2,1,0:T(8,128)(2,1)S(1)}, u32[]{:S(2)}, u32[]{:S(2)}) async-start(bf16[32,1,32,128]{3,2,1,0:T(8,128)(2,1)} %broadcast_in_dim.109), calls=%async_computation | async-start | bytes 524288 | tf_op jit(solution)/shard_map/all_to_all | solution.py:114
  20.0 0.7 %copy-start.5 = (f32[24,1,256]{2,1,0:T(1,128)S(1)}, f32[24,1,256]{2,1,0:T(1,128)}, u32[]{:S(2)}) copy-start(f32[24,1,256]{2,1,0:T(1,128)} %broadcast_in_dim.113.cnt_ref) | copy-start | bytes 73732
  20.7 0.7 %copy-start.6 = (f32[24,1,256]{2,1,0:T(1,128)S(1)}, f32[24,1,256]{2,1,0:T(1,128)}, u32[]{:S(2)}) copy-start(f32[24,1,256]{2,1,0:T(1,128)} %broadcast_in_dim.117.sum_ref) | copy-start | bytes 73732
  38.9 4.6 %copy-start = (bf16[24,1024,256]{2,1,0:T(8,128)(2,1)}, bf16[24,1024,256]{2,1,0:T(8,128)(2,1)S(1)}, u32[]{:S(2)}) copy-start(bf16[24,1024,256]{2,1,0:T(8,128)(2,1)S(1)} %get-tuple-element.8.slope_ref) | copy-start | bytes 37748740
  43.4 0.7 %copy-start.3 = (bf16[32,32,128]{2,1,0:T(8,128)(2,1)}, bf16[32,32,128]{2,1,0:T(8,128)(2,1)S(1)}, u32[]{:S(2)}) copy-start(bf16[32,32,128]{2,1,0:T(8,128)(2,1)S(1)} %get-tuple-element.7) | copy-start | bytes 786436
  44.2 0.6 copy-start.4
  44.8 17.8 %all-to-all-start.1 = ((bf16[32,1,32,128]{3,2,1,0:T(8,128)(2,1)}), bf16[32,1,32,128]{3,2,1,0:T(8,128)(2,1)S(1)}, u32[]{:S(2)}, u32[]{:S(2)}) async-start(bf16[32,1,32,128]{3,2,1,0:T(8,128)(2,1)} %bitcast.12), calls=%async_computation.1 | async-start | bytes 524288 | tf_op jit(solution)/shard_map/all_to_all | solution.py:162
  53.4 4.6 %copy-start.1 = (bf16[24,1024,256]{2,1,0:T(8,128)(2,1)S(1)}, bf16[24,1024,256]{2,1,0:T(8,128)(2,1)}, u32[]{:S(2)}) copy-start(bf16[24,1024,256]{2,1,0:T(8,128)(2,1)} %copy-done) | copy-start | bytes 37748740

commit v2 on v1

v2 whole, which is shorter than its diff:
```python
import jax
import jax.numpy as jnp
from jax import lax
from jax.experimental import pallas as pl
from jax.experimental.pallas import tpu as pltpu
from jax.sharding import PartitionSpec as P

AXES = ("group", "member")
BLOCK = 8
LANES = 128
INV_TEMP = 20.0
LOG2E = 1.4426950408889634


def plan_kernel(count, users_ref, teacher_ref, table_ref, place_ref, cnt_ref, aim_ref):
    n_pages, slots = users_ref.shape
    width = cnt_ref.shape[2]
    per_page = cnt_ref.shape[0] // n_pages
    n_tok = width // BLOCK
    square = (LANES, LANES)
    pad = jnp.zeros((LANES - n_pages, slots), jnp.float32)
    side = jnp.zeros((LANES, LANES - slots), jnp.float32)
    wide = jnp.concatenate(
        [jnp.concatenate([users_ref[...].astype(jnp.float32), pad], axis=0), side], axis=1)
    tall = wide.T
    row = lax.broadcasted_iota(jnp.int32, (slots, LANES), 0)
    col = lax.broadcasted_iota(jnp.int32, (slots, LANES), 1)
    colf = col.astype(jnp.float32)
    teach = jnp.concatenate([teacher_ref[...], jnp.zeros((n_pages, LANES - slots), jnp.float32)], axis=1)
    spread_k = lax.broadcasted_iota(jnp.int32, (slots, slots * n_tok), 0)
    spread_l = lax.broadcasted_iota(jnp.int32, (slots, slots * n_tok), 1)
    spread = jnp.where((spread_l >= spread_k * n_tok) & (spread_l < (spread_k + 1) * n_tok), 1.0, 0.0)
    for p in range(n_pages):
        total = count[p]
        ucol = tall[0:slots, p:p + 1]
        urow = wide[p:p + 1, :]
        alive = (row < total) & (col < total)
        same = jnp.where((ucol == urow) & alive, 1.0, 0.0)
        before_c = jnp.sum(jnp.where(col < row, same, 0.0), axis=1, keepdims=True)
        before_r = jnp.sum(jnp.where(row < col, same, 0.0), axis=0, keepdims=True)
        first_c = (before_c == 0.0) & (row[:, 0:1] < total)
        first_r = (before_r == 0.0) & (col[0:1, :] < total)
        first_cf = jnp.where(first_c, 1.0, 0.0)
        first_rf = jnp.where(first_r, 1.0, 0.0)
        rank_c = jnp.sum(jnp.where(col < row, first_rf, 0.0), axis=1, keepdims=True)
        number = jnp.sum(first_rf, axis=1, keepdims=True)
        put = jnp.where(rank_c == colf, first_cf, 0.0)
        order = jnp.sum(put * ucol, axis=0, keepdims=True)
        hits = jnp.sum(same, axis=1, keepdims=True)
        aims = jnp.sum(same * teach[p:p + 1, :], axis=1, keepdims=True)
        cnt = jnp.sum(put * hits, axis=0, keepdims=True)
        aim = jnp.sum(put * aims, axis=0, keepdims=True)
        place = jnp.sum(same * (first_cf * rank_c), axis=0, keepdims=True)
        blocks = jnp.floor((number + (BLOCK - 1)) * (1.0 / BLOCK))
        entry = jnp.where(col[0:1, :] == slots, blocks, order)
        table_ref[p:p + 1, :] = entry.astype(jnp.int32)
        place_ref[p:p + 1, :] = jnp.where(col[0:1, :] < total, place, -1.0).astype(jnp.int32)
        both = jnp.concatenate([cnt, aim, jnp.zeros((6, LANES), jnp.float32)], axis=0)[:, 0:slots]
        lanes = jnp.dot(both, spread, precision=lax.Precision.HIGHEST,
                        preferred_element_type=jnp.float32)
        for j in range(per_page):
            cnt_ref[p * per_page + j] = lanes[0:1, j * width:(j + 1) * width]
            aim_ref[p * per_page + j] = lanes[1:2, j * width:(j + 1) * width]


def grad_kernel(table, q_ref, page_ref, page_t_ref, cnt_ref, aim_ref, place_ref,
                dq_hbm, slope_hbm, score_hbm,
                q2, qb, diag, sim, wts, moved, slope, acc, dq, shown, stat, sems, out_sem):
    n_pages, p_tok, dim = page_ref.shape
    n_tok = q_ref.shape[1]
    width = BLOCK * n_tok
    per_page = slope_hbm.shape[0] // n_pages
    slots = per_page * BLOCK
    chunk = 64
    parts = range(0, p_tok, chunk)
    scale_in = INV_TEMP * LOG2E
    share = 4
    quarters = p_tok // (share * chunk)
    always = table[0, slots] > 0

    def fold(x, op):
        x = x.reshape(x.shape[0] // 8, 8, width)
        out = x[0]
        for i in range(1, x.shape[0]):
            out = op(out, x[i])
        return out

    def flip(p, j):
        more = j + 1 < table[p, slots]
        last = p + 1 >= n_pages
        p2 = jnp.where(more, p, jnp.where(last, p, p + 1))
        j2 = jnp.where(more, j + 1, jnp.where(last, j, 0))
        return p2, j2

    def load_block(p, j):
        for k in range(BLOCK):
            qb[pl.ds(k * n_tok, n_tok), :] = q2[table[p, j * BLOCK + k]]

    def similar(p, n, top):
        rows = share * chunk
        tile = page_ref[p, n * rows:(n + 1) * rows, :]
        both = jnp.concatenate([tile, tile], axis=1)
        s = lax.dot_general(both, qb[...], (((1,), (1,)), ((), ())), preferred_element_type=jnp.float32)
        sim[n * rows:(n + 1) * rows, :] = s
        most = fold(s, jnp.maximum)
        return most if top is None else jnp.maximum(top, most)

    def add_part(p, j, part):
        part = part.T
        for k in range(BLOCK):
            acc[table[p, j * BLOCK + k]] += part[k * n_tok:(k + 1) * n_tok, :]

    def out_copy(b, slot):
        return pltpu.make_async_copy(slope.at[slot], slope_hbm.at[b], sems.at[slot])

    acc[...] = jnp.zeros_like(acc)
    shown[...] = jnp.zeros_like(shown)
    slope[1] = jnp.zeros((p_tok, width), slope.dtype)
    lane_i = lax.broadcasted_iota(jnp.int32, (width, width), 0) // n_tok
    lane_j = lax.broadcasted_iota(jnp.int32, (width, width), 1) // n_tok
    diag[...] = jnp.where(lane_i == lane_j, 1.0, 0.0).astype(jnp.bfloat16)
    wide = q_ref[...].astype(jnp.float32) * scale_in
    hi = wide.astype(jnp.bfloat16)
    q2[:, :, 0:dim] = hi
    q2[:, :, dim:2 * dim] = (wide - hi.astype(jnp.float32)).astype(jnp.bfloat16)
    load_block(0, 0)
    top = None
    for n in range(quarters):
        top = similar(0, n, top)
    stat[0] = top

    def step(t, carry):
        p0, j0, p, j = carry
        p2, j2 = flip(p, j)
        slot = lax.rem(t, 2)
        b = p * per_page + j

        @pl.when(always)
        def _():
            top = jnp.max(stat[0], axis=0, keepdims=True)
            total = jnp.zeros((8, width), jnp.float32)
            mass = jnp.zeros((8, width), jnp.float32)
            part = None
            for n, i in enumerate(parts):
                if n % share == 0:
                    k = n * chunk
                    term = jnp.dot(page_t_ref[p0, :, k:k + share * chunk], slope[1 - slot, k:k + share * chunk, :],
                                   preferred_element_type=jnp.float32)
                    part = term if part is None else part + term
                r = pl.ds(i, chunk)
                d = sim[r, :] - top
                e = jnp.exp2(d)
                v = e * d
                wts[r, :] = e
                moved[r, :] = v
                total += fold(e, jnp.add)
                mass += fold(v, jnp.add)
            add_part(p0, j0, part)
            stat[1] = total
            stat[2] = mass
            stat[3] = jnp.broadcast_to(top, (8, width))

        @pl.when(t >= 2)
        def _():
            out_copy(b, slot).wait()

        @pl.when(always)
        def _():
            inv = 1.0 / jnp.sum(stat[1], axis=0, keepdims=True)
            drift = jnp.sum(stat[2], axis=0, keepdims=True) * inv
            matched = (stat[3, 0:1, :] + drift) * (1.0 / scale_in)
            load_block(p2, j2)
            ahead = quarters // 2
            high = None
            for n in range(ahead):
                high = similar(p2, n, high)
            hi = matched.astype(jnp.bfloat16)
            rest = matched - hi.astype(jnp.float32)
            mid = rest.astype(jnp.bfloat16)
            low = (rest - mid.astype(jnp.float32)).astype(jnp.bfloat16)
            pieces = jnp.concatenate([hi, mid, low], axis=0)
            score = jnp.sum(
                jnp.dot(pieces, diag[...], preferred_element_type=jnp.float32), axis=0, keepdims=True)
            place = place_ref[pl.ds(p, 1), :]
            line = shown[pl.ds(p, 1), :]
            for k in range(BLOCK):
                part = score[:, (k * n_tok // LANES) * LANES:(k * n_tok // LANES + 1) * LANES]
                off = k * n_tok % LANES
                if off:
                    part = pltpu.roll(part, LANES - off, 1)
                line = jnp.where(place == j * BLOCK + k, part, line)
            shown[pl.ds(p, 1), :] = line
            scale = (cnt_ref[b] * score - aim_ref[b]) * inv
            beta = scale * (1.0 / LOG2E)
            alpha = scale - beta * drift
            for n, i in enumerate(parts):
                if n % share == 0 and n // share < quarters - ahead:
                    high = similar(p2, ahead + n // share, high)
                r = pl.ds(i, chunk)
                slope[slot, r, :] = (alpha * wts[r, :] + beta * moved[r, :]).astype(jnp.bfloat16)

            stat[0] = high

        out_copy(b, slot).start()
        return p, j, p2, j2

    count = table[0, slots]
    for p in range(1, n_pages):
        count += table[p, slots]
    zero = jnp.int32(0)
    p, j, _, _ = lax.fori_loop(0, count, step, (zero, zero, zero, zero))
    add_part(p, j, jnp.dot(page_t_ref[p], slope[lax.rem(count - 1, 2)], preferred_element_type=jnp.float32))
    dq[...] = acc[...].astype(dq.dtype)
    dq_copy = pltpu.make_async_copy(dq, dq_hbm, out_sem.at[0])
    score_copy = pltpu.make_async_copy(shown, score_hbm, out_sem.at[1])
    dq_copy.start()
    score_copy.start()
    out_copy(0, 0).wait()
    out_copy(0, 1).wait()
    dq_copy.wait()
    score_copy.wait()


def page_kernel(table, q_ref, slope_hbm, out_hbm, qb, buf, out, sems, out_sems):
    n_pages, p_tok, dim = out_hbm.shape
    n_tok = q_ref.shape[1]
    width = BLOCK * n_tok
    per_page = slope_hbm.shape[0] // n_pages
    slots = per_page * BLOCK

    def fetch(p, j):
        return pltpu.make_async_copy(
            slope_hbm.at[p * per_page + j], buf.at[p % 2, j], sems.at[p % 2, j])

    def store(p):
        return pltpu.make_async_copy(out.at[p % 2], out_hbm.at[p], out_sems.at[p % 2])

    def start(p):
        for j in range(per_page):
            @pl.when(j < table[p, slots])
            def _():
                fetch(p, j).start()

    start(0)
    for p in range(n_pages):
        if p + 1 < n_pages:
            start(p + 1)
        if p >= 2:
            store(p - 2).wait()
        for k in range(slots):
            qb[pl.ds(k * n_tok, n_tok), :] = q_ref[table[p, k]]
        for n in range(1, per_page + 1):
            @pl.when(table[p, slots] == n)
            def _():
                total = None
                for j in range(n):
                    fetch(p, j).wait()
                    term = jnp.dot(buf[p % 2, j], qb[pl.ds(j * width, width), :],
                                   preferred_element_type=jnp.float32)
                    total = term if total is None else total + term
                out[p % 2] = total.astype(out.dtype)
        store(p).start()
    for p in range(max(n_pages - 2, 0), n_pages):
        store(p).wait()


def body(queries, pages, users, page_count, teacher):
    n_dev = lax.axis_size("group") * lax.axis_size("member")
    own, n_tok, dim = queries.shape
    n_pages, p_tok, _ = pages.shape
    slots = users.shape[1]
    n_query = n_dev * own
    per_page = slots // BLOCK
    n_blocks = n_pages * per_page
    width = BLOCK * n_tok
    smem = pl.BlockSpec(memory_space=pltpu.SMEM)
    vmem = pl.BlockSpec(memory_space=pltpu.VMEM)
    hbm = pl.BlockSpec(memory_space=pl.ANY)

    copies = jnp.broadcast_to(queries[None], (n_dev, own, n_tok, dim))
    gathered = lax.all_to_all(copies, AXES, split_axis=0, concat_axis=0, tiled=True)
    gathered = gathered.reshape(n_query, n_tok, dim)
    page_t = jnp.swapaxes(pages, 1, 2)

    table, place, cnt, aim = pl.pallas_call(
        plan_kernel,
        out_shape=(
            jax.ShapeDtypeStruct((n_pages, LANES), jnp.int32),
            jax.ShapeDtypeStruct((n_pages, LANES), jnp.int32),
            jax.ShapeDtypeStruct((n_blocks, 1, width), jnp.float32),
            jax.ShapeDtypeStruct((n_blocks, 1, width), jnp.float32),
        ),
        in_specs=[smem, vmem, vmem],
        out_specs=(vmem,) * 4,
        compiler_params=pltpu.CompilerParams(vmem_limit_bytes=16 << 20),
        cost_estimate=pl.CostEstimate(flops=10**6, bytes_accessed=1 << 16, transcendentals=0),
        name="plan",
    )(page_count, users, teacher)

    dq, slope, scores = pl.pallas_call(
        grad_kernel,
        out_shape=(
            jax.ShapeDtypeStruct((n_query, n_tok, dim), jnp.bfloat16),
            jax.ShapeDtypeStruct((n_blocks, p_tok, width), jnp.bfloat16),
            jax.ShapeDtypeStruct((n_pages, LANES), jnp.float32),
        ),
        in_specs=[smem] + [vmem] * 6,
        out_specs=(hbm, hbm, hbm),
        scratch_shapes=[
            pltpu.VMEM((n_query, n_tok, 2 * dim), jnp.bfloat16),
            pltpu.VMEM((width, 2 * dim), jnp.bfloat16),
            pltpu.VMEM((width, width), jnp.bfloat16),
            pltpu.VMEM((p_tok, width), jnp.float32),
            pltpu.VMEM((p_tok, width), jnp.float32),
            pltpu.VMEM((p_tok, width), jnp.float32),
            pltpu.VMEM((2, p_tok, width), jnp.bfloat16),
            pltpu.VMEM((n_query, n_tok, dim), jnp.float32),
            pltpu.VMEM((n_query, n_tok, dim), jnp.bfloat16),
            pltpu.VMEM((n_pages, LANES), jnp.float32),
            pltpu.VMEM((4, 8, width), jnp.float32),
            pltpu.SemaphoreType.DMA((2,)),
            pltpu.SemaphoreType.DMA((2,)),
        ],
        compiler_params=pltpu.CompilerParams(vmem_limit_bytes=48 << 20),
        cost_estimate=pl.CostEstimate(flops=4 * 10**9, bytes_accessed=16 << 20, transcendentals=4 << 20),
        name="grad",
    )(table, gathered, pages, page_t, cnt, aim, place)

    terms = lax.all_to_all(
        dq.reshape(n_dev, own, n_tok, dim), AXES, split_axis=0, concat_axis=0, tiled=True)

    page_grad = pl.pallas_call(
        page_kernel,
        out_shape=jax.ShapeDtypeStruct(pages.shape, pages.dtype),
        in_specs=[smem, vmem, hbm],
        out_specs=hbm,
        scratch_shapes=[
            pltpu.VMEM((slots * n_tok, dim), jnp.bfloat16),
            pltpu.VMEM((2, per_page, p_tok, width), jnp.bfloat16),
            pltpu.VMEM((2, p_tok, dim), jnp.bfloat16),
            pltpu.SemaphoreType.DMA((2, per_page)),
            pltpu.SemaphoreType.DMA((2,)),
        ],
        compiler_params=pltpu.CompilerParams(vmem_limit_bytes=48 << 20),
        cost_estimate=pl.CostEstimate(flops=2 * 10**9, bytes_accessed=16 << 20, transcendentals=0),
        name="page_part",
    )(table, gathered, slope)

    query_grad = jnp.sum(terms.astype(jnp.float32), axis=0)
    return scores[:, :slots], query_grad, page_grad


def solution(mesh):
    return jax.shard_map(
        body,
        mesh=mesh,
        in_specs=(P(AXES, None, None), P(AXES, None, None), P(AXES, None), P(AXES), P(AXES, None)),
        out_specs=(P(AXES, None), P(AXES, None, None), P(AXES, None, None)),
        check_vma=False,
    )
```

time: 64.5 us -> 49.6 us (0.77)
  local copies, waits for them, and re-layouts: 16.1 us -> 4 us
  other arithmetic: 9.54 us -> 0.65 us
  waiting for transfers between devices: 0.65 us -> 9.19 us
  starting transfers between devices: 14.1 us -> 10.5 us
  Pallas kernels: 22 us -> 23.6 us
    unnamed x16 -> x11, local copies, waits for them, and re-layouts: 12.7 us -> 2.56 us
    all_to_all x1, waiting for transfers between devices: 0.65 us -> 6.94 us  [body(): lax.all_to_all(copies, AXES, split_axis=0, concat_axis=0, tiled=True)]
    pallas_call x1, Pallas kernels: 17.4 us -> 13.8 us  [body(): pl.pallas_call(grad_kernel, out_shape=(jax.ShapeDtypeStruct((n_query, n_t...]
    all_to_all x1, starting transfers between devices: 6.79 us -> 3.19 us  [body(): lax.all_to_all(dq.reshape(n_dev, own, n_tok, dim), AXES, split_axis=0, co...]
    pallas_call x1, Pallas kernels: 4.6 us -> 8.19 us  [body(): pl.pallas_call(page_kernel, out_shape=jax.ShapeDtypeStruct(pages.shape, p...]
    broadcast_in_dim x2 -> x0, other arithmetic: 3.28 us -> none  [the longest x1 1.64 us: body(): aim = jnp.sum(jnp.where(put, aims[:, :, None], 0.0), axis=1)]
    reduce_sum x4 -> x0, other arithmetic: 2.92 us -> none  [the longest x1 1.08 us: body(): jnp.sum(jnp.where(same & first[:, None, :], rank[:, None, :], 0), axis=2)]
    all_to_all x1, waiting for transfers between devices: 0.01 us -> 2.25 us  [body(): lax.all_to_all(dq.reshape(n_dev, own, n_tok, dim), AXES, split_axis=0, co...]
  transfers between devices with their start and end apart: 2 -> 2, of which waited for: 1 -> 2; matrix products, arithmetic and copies ran while one was open for 18% -> 4% of each run, Pallas kernels for 7% -> 20%
where the time goes in v2:
time: 49.6 us; the launch traced here: 48.7 us
  Pallas kernels  23.6 us (48%)
  starting transfers between devices  10.5 us (21%)
  waiting for transfers between devices  9.19 us (19%)
  local copies, waits for them, and re-layouts  4 us (8%)
  between operations  0.74 us (1%)
  other arithmetic  0.65 us (1%)
    pallas_call x1, Pallas kernels, body(): pl.pallas_call(grad_kernel, out_shape=(jax.ShapeDtypeStruct((n_query, n_t...  13.8 us
    pallas_call x1, Pallas kernels, body(): pl.pallas_call(page_kernel, out_shape=jax.ShapeDtypeStruct(pages.shape, p...  8.19 us
    all_to_all x1, starting transfers between devices, body(): lax.all_to_all(copies, AXES, split_axis=0, concat_axis=0, tiled=True)  7.33 us
    all_to_all x1, waiting for transfers between devices, body(): lax.all_to_all(copies, AXES, split_axis=0, concat_axis=0, tiled=True)  6.94 us
    all_to_all x1, starting transfers between devices, body(): lax.all_to_all(dq.reshape(n_dev, own, n_tok, dim), AXES, split_axis=0, co...  3.19 us
    unnamed x11, local copies, waits for them, and re-layouts  2.56 us
    all_to_all x1, waiting for transfers between devices, body(): lax.all_to_all(dq.reshape(n_dev, own, n_tok, dim), AXES, split_axis=0, co...  2.25 us
    pallas_call x1, Pallas kernels, body(): pl.pallas_call(plan_kernel, out_shape=(jax.ShapeDtypeStruct((n_pages, LAN...  1.58 us
  transfers between devices with their start and end apart: 2, of which 2 were waited for; matrix products, arithmetic and copies ran while one was open for 4% of the time, Pallas kernels for 20%

profile of v2, /device:TPU:0, one launch (start us, length us, event | category | flops | bytes accessed | tf_op | source)
XLA Modules:
  0.0 48.7 jit_solution(17232397952183855205)
XLA Ops:
  0.6 1.4 %broadcast_in_dim.9 = bf16[32,1,32,128]{3,2,1,0:T(8,128)(2,1)} broadcast(bf16[32,128]{1,0:T(8,128)(2,1)} %bitcast.13), dimensions={2,3} | broadcast | bytes 270336 | tf_op jit(solution)/shard_map/broadcast_in_dim | solution.py:280
  2.1 7.3 %all-to-all-start = ((bf16[32,1,32,128]{3,2,1,0:T(8,128)(2,1)}), bf16[32,1,32,128]{3,2,1,0:T(8,128)(2,1)S(1)}, u32[]{:S(2)}, u32[]{:S(2)}) async-start(bf16[32,1,32,128]{3,2,1,0:T(8,128)(2,1)} %broadcast_in_dim.9), calls=%async_computation | async-start | bytes 524288 | tf_op jit(solution)/shard_map/all_to_all | solution.py:281
  9.4 0.0 copy-start.2
  9.4 0.0 copy-start.3
  9.4 0.0 copy-start.4
  9.4 0.0 copy-start
  9.4 1.8 %copy.9 = bf16[6,1024,128]{1,2,0:T(8,128)(2,1)S(1)} copy(bf16[6,1024,128]{2,1,0:T(8,128)(2,1)} %page_ref.1) | data formatting | bytes 3145728 | tf_op args[1]
  11.3 0.0 copy-done.2
  11.3 0.0 copy-done.3
  11.3 0.0 copy-done.4
  11.3 1.6 %plan.1 = (s32[6,128]{1,0:T(8,128)S(1)}, s32[6,128]{1,0:T(8,128)S(1)}, f32[24,1,256]{2,1,0:T(1,128)S(1)}, f32[24,1,256]{2,1,0:T(1,128)S(1)}) custom-call(s32[6]{0:T(128)S(1)} %copy-done.4, s32[6,32]{1,0:T(8,128)S(1)} %copy-done.2, f32[6,32]{1,0:T(8,128)S(1)} %copy-done.3), custom_call_target="tpu_custom_call" | custom-call | flops 1000000 | bytes 65536 | tf_op jit(solution)/shard_map/plan/pallas_call | solution.py:285
  12.9 6.9 %all-to-all-done = bf16[32,1,32,128]{3,2,1,0:T(8,128)(2,1)S(1)} async-done(((bf16[32,1,32,128]{3,2,1,0:T(8,128)(2,1)}), bf16[32,1,32,128]{3,2,1,0:T(8,128)(2,1)S(1)}, u32[]{:S(2)}, u32[]{:S(2)}) %all-to-all-start) | async-done | bytes 262176 | tf_op jit(solution)/shard_map/all_to_all | solution.py:281
  19.8 0.0 copy-done
  19.8 13.8 %grad.1 = (bf16[32,32,128]{2,1,0:T(8,128)(2,1)S(1)}, bf16[24,1024,256]{2,1,0:T(8,128)(2,1)}, f32[6,128]{1,0:T(8,128)}) custom-call(s32[6,128]{1,0:T(8,128)S(1)} %get-tuple-element.10.table, bf16[32,32,128]{2,1,0:T(8,128)(2,1)S(1)} %bitcast.9, bf16[6,1024,128]{2,1,0:T(8,128)(2,1)S(1)} %copy-done, bf16[6,128,1024]{2,1,0:T(8,128)(2,1)S(1)} %bitcast.8, ...), custom_call_target="tpu_custom_call" | custom-call | flops 4000000000 | bytes 16777216 | tf_op jit(solution)/shard_map/grad/pallas_call | solution.py:300
  33.7 0.0 copy-start.1
  33.7 0.7 %copy-done.1 = bf16[32,32,128]{2,1,0:T(8,128)(2,1)} copy-done((bf16[32,32,128]{2,1,0:T(8,128)(2,1)}, bf16[32,32,128]{2,1,0:T(8,128)(2,1)S(1)}, u32[]{:S(2)}) %copy-start.1) | copy-done | bytes 262168
  34.4 3.2 %all-to-all-start.1 = ((bf16[32,1,32,128]{3,2,1,0:T(8,128)(2,1)}), bf16[32,1,32,128]{3,2,1,0:T(8,128)(2,1)S(1)}, u32[]{:S(2)}, u32[]{:S(2)}) async-start(bf16[32,1,32,128]{3,2,1,0:T(8,128)(2,1)} %bitcast.11), calls=%async_computation.1 | async-start | bytes 524288 | tf_op jit(solution)/shard_map/all_to_all | solution.py:329
  37.6 8.2 %page_part.1 = bf16[6,1024,128]{2,1,0:T(8,128)(2,1)} custom-call(s32[6,128]{1,0:T(8,128)S(1)} %get-tuple-element.10.table, bf16[32,32,128]{2,1,0:T(8,128)(2,1)S(1)} %bitcast.10, bf16[24,1024,256]{2,1,0:T(8,128)(2,1)} %get-tuple-element.16.slope_hbm), custom_call_target="tpu_custom_call" | custom-call | flops 2000000000 | bytes 16777216 | tf_op jit(solution)/shard_map/page_part/pallas_call | solution.py:332
  45.8 2.2 %all-to-all-done.1 = bf16[32,1,32,128]{3,2,1,0:T(8,128)(2,1)S(1)} async-done(((bf16[32,1,32,128]{3,2,1,0:T(8,128)(2,1)}), bf16[32,1,32,128]{3,2,1,0:T(8,128)(2,1)S(1)}, u32[]{:S(2)}, u32[]{:S(2)}) %all-to-all-start.1) | async-done | bytes 262176 | tf_op jit(solution)/shard_map/all_to_all | solution.py:329
  48.0 0.7 %convert_reduce_fusion = f32[32,128]{1,0:T(8,128)} fusion(bf16[32,1,32,128]{3,2,1,0:T(8,128)(2,1)S(1)} %all-to-all-done.1), kind=kLoop, calls=%fused_computation | loop fusion | flops 258048 | bytes 278528 | tf_op jit(solution)/shard_map/reduce_sum | solution.py:349
Async XLA Ops:
  2.1 17.8 %all-to-all-start = ((bf16[32,1,32,128]{3,2,1,0:T(8,128)(2,1)}), bf16[32,1,32,128]{3,2,1,0:T(8,128)(2,1)S(1)}, u32[]{:S(2)}, u32[]{:S(2)}) async-start(bf16[32,1,32,128]{3,2,1,0:T(8,128)(2,1)} %broadcast_in_dim.9), calls=%async_computation | async-start | bytes 524288 | tf_op jit(solution)/shard_map/all_to_all | solution.py:281
  9.4 1.9 %copy-start.2 = (s32[6,32]{1,0:T(8,128)S(1)}, s32[6,32]{1,0:T(8,128)}, u32[]{:S(2)}) copy-start(s32[6,32]{1,0:T(8,128)} %users_ref.1) | copy-start | bytes 2308
  9.4 1.9 %copy-start.3 = (f32[6,32]{1,0:T(8,128)S(1)}, f32[6,32]{1,0:T(8,128)}, u32[]{:S(2)}) copy-start(f32[6,32]{1,0:T(8,128)} %teacher_ref.1) | copy-start | bytes 2308
  9.4 1.9 %copy-start.4 = (s32[6]{0:T(128)S(1)}, s32[6]{0:T(128)}, u32[]{:S(2)}) copy-start(s32[6]{0:T(128)} %count.1) | copy-start | bytes 76
  9.4 10.4 %copy-start = (bf16[6,1024,128]{2,1,0:T(8,128)(2,1)S(1)}, bf16[6,1024,128]{2,1,0:T(8,128)(2,1)}, u32[]{:S(2)}) copy-start(bf16[6,1024,128]{2,1,0:T(8,128)(2,1)} %page_ref.1) | copy-start | bytes 4718596
  33.7 0.7 %copy-start.1 = (bf16[32,32,128]{2,1,0:T(8,128)(2,1)}, bf16[32,32,128]{2,1,0:T(8,128)(2,1)S(1)}, u32[]{:S(2)}) copy-start(bf16[32,32,128]{2,1,0:T(8,128)(2,1)S(1)} %get-tuple-element.15) | copy-start | bytes 786436
  34.4 13.6 %all-to-all-start.1 = ((bf16[32,1,32,128]{3,2,1,0:T(8,128)(2,1)}), bf16[32,1,32,128]{3,2,1,0:T(8,128)(2,1)S(1)}, u32[]{:S(2)}, u32[]{:S(2)}) async-start(bf16[32,1,32,128]{3,2,1,0:T(8,128)(2,1)} %bitcast.11), calls=%async_computation.1 | async-start | bytes 524288 | tf_op jit(solution)/shard_map/all_to_all | solution.py:329

commit v3 on v2

--- a/solution.py
+++ b/solution.py
@@ -115,14 +115,18 @@
 
     acc[...] = jnp.zeros_like(acc)
     shown[...] = jnp.zeros_like(shown)
-    slope[1] = jnp.zeros((p_tok, width), slope.dtype)
     lane_i = lax.broadcasted_iota(jnp.int32, (width, width), 0) // n_tok
     lane_j = lax.broadcasted_iota(jnp.int32, (width, width), 1) // n_tok
     diag[...] = jnp.where(lane_i == lane_j, 1.0, 0.0).astype(jnp.bfloat16)
-    wide = q_ref[...].astype(jnp.float32) * scale_in
-    hi = wide.astype(jnp.bfloat16)
-    q2[:, :, 0:dim] = hi
-    q2[:, :, dim:2 * dim] = (wide - hi.astype(jnp.float32)).astype(jnp.bfloat16)
+
+    def split_step(i, c):
+        for k in range(BLOCK):
+            wide = q_ref[i * BLOCK + k].astype(jnp.float32) * scale_in
+            hi = wide.astype(jnp.bfloat16)
+            q2[i * BLOCK + k, :, 0:dim] = hi
+            q2[i * BLOCK + k, :, dim:2 * dim] = (wide - hi.astype(jnp.float32)).astype(jnp.bfloat16)
+        return c
+    lax.fori_loop(0, q_ref.shape[0] // BLOCK, split_step, 0)
     load_block(0, 0)
     top = None
     for n in range(quarters):
@@ -155,7 +159,7 @@
                 moved[r, :] = v
                 total += fold(e, jnp.add)
                 mass += fold(v, jnp.add)
-            add_part(p0, j0, part)
+            add_part(p0, j0, jnp.where(t >= 1, part, 0.0))
             stat[1] = total
             stat[2] = mass
             stat[3] = jnp.broadcast_to(top, (8, width))
@@ -170,7 +174,7 @@
             drift = jnp.sum(stat[2], axis=0, keepdims=True) * inv
             matched = (stat[3, 0:1, :] + drift) * (1.0 / scale_in)
             load_block(p2, j2)
-            ahead = quarters // 2
+            ahead = 1
             high = None
             for n in range(ahead):
                 high = similar(p2, n, high)
@@ -197,8 +201,9 @@
                 if n % share == 0 and n // share < quarters - ahead:
                     high = similar(p2, ahead + n // share, high)
                 r = pl.ds(i, chunk)
-                slope[slot, r, :] = (alpha * wts[r, :] + beta * moved[r, :]).astype(jnp.bfloat16)
-
+                y = alpha * wts[r, :] + beta * moved[r, :]
+                slope[slot, r, :] = y.astype(jnp.bfloat16)
+            stat[4] = high + y[0:8, :]
             stat[0] = high
 
         out_copy(b, slot).start()
@@ -228,40 +233,43 @@
     per_page = slope_hbm.shape[0] // n_pages
     slots = per_page * BLOCK
 
-    def fetch(p, j):
-        return pltpu.make_async_copy(
-            slope_hbm.at[p * per_page + j], buf.at[p % 2, j], sems.at[p % 2, j])
-
-    def store(p):
-        return pltpu.make_async_copy(out.at[p % 2], out_hbm.at[p], out_sems.at[p % 2])
-
-    def start(p):
+    def fetch(b):
+        return pltpu.make_async_copy(slope_hbm.at[b], buf.at[b], sems.at[b])
+
+    def store(p, slot):
+        return pltpu.make_async_copy(out.at[slot], out_hbm.at[p], out_sems.at[slot])
+
+    for p in range(n_pages):
         for j in range(per_page):
             @pl.when(j < table[p, slots])
             def _():
-                fetch(p, j).start()
-
-    start(0)
-    for p in range(n_pages):
-        if p + 1 < n_pages:
-            start(p + 1)
-        if p >= 2:
-            store(p - 2).wait()
-        for k in range(slots):
-            qb[pl.ds(k * n_tok, n_tok), :] = q_ref[table[p, k]]
+                fetch(p * per_page + j).start()
+
+    def page_step(p, c):
+        slot = lax.rem(p, 2)
+        number = table[p, slots]
+
+        @pl.when(p >= 2)
+        def _():
+            store(p, slot).wait()
         for n in range(1, per_page + 1):
-            @pl.when(table[p, slots] == n)
+            @pl.when(number == n)
             def _():
                 total = None
+                for k in range(n * BLOCK):
+                    qb[pl.ds(k * n_tok, n_tok), :] = q_ref[table[p, k]]
                 for j in range(n):
-                    fetch(p, j).wait()
-                    term = jnp.dot(buf[p % 2, j], qb[pl.ds(j * width, width), :],
+                    fetch(p * per_page + j).wait()
+                for j in range(n):
+                    term = jnp.dot(buf[p * per_page + j], qb[pl.ds(j * width, width), :],
                                    preferred_element_type=jnp.float32)
                     total = term if total is None else total + term
-                out[p % 2] = total.astype(out.dtype)
-        store(p).start()
+                out[slot] = total.astype(out.dtype)
+        store(p, slot).start()
+        return c
+    lax.fori_loop(0, n_pages, page_step, 0)
     for p in range(max(n_pages - 2, 0), n_pages):
-        store(p).wait()
+        store(p, p % 2).wait()
 
 
 def body(queries, pages, users, page_count, teacher):
@@ -317,7 +325,7 @@
             pltpu.VMEM((n_query, n_tok, dim), jnp.float32),
             pltpu.VMEM((n_query, n_tok, dim), jnp.bfloat16),
             pltpu.VMEM((n_pages, LANES), jnp.float32),
-            pltpu.VMEM((4, 8, width), jnp.float32),
+            pltpu.VMEM((6, 8, width), jnp.float32),
             pltpu.SemaphoreType.DMA((2,)),
             pltpu.SemaphoreType.DMA((2,)),
         ],
@@ -336,9 +344,9 @@
         out_specs=hbm,
         scratch_shapes=[
             pltpu.VMEM((slots * n_tok, dim), jnp.bfloat16),
-            pltpu.VMEM((2, per_page, p_tok, width), jnp.bfloat16),
+            pltpu.VMEM((n_blocks, p_tok, width), jnp.bfloat16),
             pltpu.VMEM((2, p_tok, dim), jnp.bfloat16),
-            pltpu.SemaphoreType.DMA((2, per_page)),
+            pltpu.SemaphoreType.DMA((n_blocks,)),
             pltpu.SemaphoreType.DMA((2,)),
         ],
         compiler_params=pltpu.CompilerParams(vmem_limit_bytes=48 << 20),

time: 49.6 us -> 46.8 us (0.944)
  Pallas kernels: 23.6 us -> 18.2 us
  waiting for transfers between devices: 9.19 us -> 11.6 us
  starting transfers between devices: 10.5 us -> 11.2 us
    pallas_call x1, Pallas kernels: 13.8 us -> 10.8 us  [body(): pl.pallas_call(grad_kernel, out_shape=(jax.ShapeDtypeStruct((n_query, n_t...]
    pallas_call x1, Pallas kernels: 8.19 us -> 5.78 us  [body(): pl.pallas_call(page_kernel, out_shape=jax.ShapeDtypeStruct(pages.shape, p...]
    all_to_all x1, waiting for transfers between devices: 2.25 us -> 4.65 us  [body(): lax.all_to_all(dq.reshape(n_dev, own, n_tok, dim), AXES, split_axis=0, co...]
    all_to_all x1, starting transfers between devices: 3.19 us -> 3.89 us  [body(): lax.all_to_all(dq.reshape(n_dev, own, n_tok, dim), AXES, split_axis=0, co...]
  transfers between devices with their start and end apart: 2 -> 2, of which waited for: 2 -> 2; matrix products, arithmetic and copies ran while one was open for 4% -> 4% of each run, Pallas kernels for 20% -> 16%
where the time goes in v3:
time: 46.8 us; the launch traced here: 46.3 us
  Pallas kernels  18.2 us (39%)
  waiting for transfers between devices  11.6 us (25%)
  starting transfers between devices  11.2 us (24%)
  local copies, waits for them, and re-layouts  4 us (9%)
  between operations  0.74 us (2%)
  other arithmetic  0.65 us (1%)
    pallas_call x1, Pallas kernels, body(): pl.pallas_call(grad_kernel, out_shape=(jax.ShapeDtypeStruct((n_query, n_t...  10.8 us
    all_to_all x1, starting transfers between devices, body(): lax.all_to_all(copies, AXES, split_axis=0, concat_axis=0, tiled=True)  7.33 us
    all_to_all x1, waiting for transfers between devices, body(): lax.all_to_all(copies, AXES, split_axis=0, concat_axis=0, tiled=True)  6.94 us
    pallas_call x1, Pallas kernels, body(): pl.pallas_call(page_kernel, out_shape=jax.ShapeDtypeStruct(pages.shape, p...  5.78 us
    all_to_all x1, waiting for transfers between devices, body(): lax.all_to_all(dq.reshape(n_dev, own, n_tok, dim), AXES, split_axis=0, co...  4.65 us
    all_to_all x1, starting transfers between devices, body(): lax.all_to_all(dq.reshape(n_dev, own, n_tok, dim), AXES, split_axis=0, co...  3.89 us
    unnamed x11, local copies, waits for them, and re-layouts  2.56 us
    pallas_call x1, Pallas kernels, body(): pl.pallas_call(plan_kernel, out_shape=(jax.ShapeDtypeStruct((n_pages, LAN...  1.58 us
  transfers between devices with their start and end apart: 2, of which 2 were waited for; matrix products, arithmetic and copies ran while one was open for 4% of the time, Pallas kernels for 16%

profile of v3, /device:TPU:0, one launch (start us, length us, event | category | flops | bytes accessed | tf_op | source)
XLA Modules:
  0.0 46.3 jit_solution(7799534325493931800)
XLA Ops:
  0.6 1.4 %broadcast_in_dim.9 = bf16[32,1,32,128]{3,2,1,0:T(8,128)(2,1)} broadcast(bf16[32,128]{1,0:T(8,128)(2,1)} %bitcast.13), dimensions={2,3} | broadcast | bytes 270336 | tf_op jit(solution)/shard_map/broadcast_in_dim | solution.py:288
  2.1 7.3 %all-to-all-start = ((bf16[32,1,32,128]{3,2,1,0:T(8,128)(2,1)}), bf16[32,1,32,128]{3,2,1,0:T(8,128)(2,1)S(1)}, u32[]{:S(2)}, u32[]{:S(2)}) async-start(bf16[32,1,32,128]{3,2,1,0:T(8,128)(2,1)} %broadcast_in_dim.9), calls=%async_computation | async-start | bytes 524288 | tf_op jit(solution)/shard_map/all_to_all | solution.py:289
  9.4 0.0 copy-start.2
  9.4 0.0 copy-start.3
  9.4 0.0 copy-start.4
  9.4 0.0 copy-start
  9.4 1.8 %copy.9 = bf16[6,1024,128]{1,2,0:T(8,128)(2,1)S(1)} copy(bf16[6,1024,128]{2,1,0:T(8,128)(2,1)} %page_ref.1) | data formatting | bytes 3145728 | tf_op args[1]
  11.3 0.0 copy-done.2
  11.3 0.0 copy-done.3
  11.3 0.0 copy-done.4
  11.3 1.6 %plan.1 = (s32[6,128]{1,0:T(8,128)S(1)}, s32[6,128]{1,0:T(8,128)S(1)}, f32[24,1,256]{2,1,0:T(1,128)S(1)}, f32[24,1,256]{2,1,0:T(1,128)S(1)}) custom-call(s32[6]{0:T(128)S(1)} %copy-done.4, s32[6,32]{1,0:T(8,128)S(1)} %copy-done.2, f32[6,32]{1,0:T(8,128)S(1)} %copy-done.3), custom_call_target="tpu_custom_call" | custom-call | flops 1000000 | bytes 65536 | tf_op jit(solution)/shard_map/plan/pallas_call | solution.py:293
  12.9 6.9 %all-to-all-done = bf16[32,1,32,128]{3,2,1,0:T(8,128)(2,1)S(1)} async-done(((bf16[32,1,32,128]{3,2,1,0:T(8,128)(2,1)}), bf16[32,1,32,128]{3,2,1,0:T(8,128)(2,1)S(1)}, u32[]{:S(2)}, u32[]{:S(2)}) %all-to-all-start) | async-done | bytes 262176 | tf_op jit(solution)/shard_map/all_to_all | solution.py:289
  19.8 0.0 copy-done
  19.8 10.8 %grad.1 = (bf16[32,32,128]{2,1,0:T(8,128)(2,1)S(1)}, bf16[24,1024,256]{2,1,0:T(8,128)(2,1)}, f32[6,128]{1,0:T(8,128)}) custom-call(s32[6,128]{1,0:T(8,128)S(1)} %get-tuple-element.10.table, bf16[32,32,128]{2,1,0:T(8,128)(2,1)S(1)} %bitcast.9, bf16[6,1024,128]{2,1,0:T(8,128)(2,1)S(1)} %copy-done, bf16[6,128,1024]{2,1,0:T(8,128)(2,1)S(1)} %bitcast.8, ...), custom_call_target="tpu_custom_call" | custom-call | flops 4000000000 | bytes 16777216 | tf_op jit(solution)/shard_map/grad/pallas_call | solution.py:308
  30.6 0.0 copy-start.1
  30.6 0.7 %copy-done.1 = bf16[32,32,128]{2,1,0:T(8,128)(2,1)} copy-done((bf16[32,32,128]{2,1,0:T(8,128)(2,1)}, bf16[32,32,128]{2,1,0:T(8,128)(2,1)S(1)}, u32[]{:S(2)}) %copy-start.1) | copy-done | bytes 262168
  31.3 3.9 %all-to-all-start.1 = ((bf16[32,1,32,128]{3,2,1,0:T(8,128)(2,1)}), bf16[32,1,32,128]{3,2,1,0:T(8,128)(2,1)S(1)}, u32[]{:S(2)}, u32[]{:S(2)}) async-start(bf16[32,1,32,128]{3,2,1,0:T(8,128)(2,1)} %bitcast.11), calls=%async_computation.1 | async-start | bytes 524288 | tf_op jit(solution)/shard_map/all_to_all | solution.py:337
  35.2 5.8 %page_part.1 = bf16[6,1024,128]{2,1,0:T(8,128)(2,1)} custom-call(s32[6,128]{1,0:T(8,128)S(1)} %get-tuple-element.10.table, bf16[32,32,128]{2,1,0:T(8,128)(2,1)S(1)} %bitcast.10, bf16[24,1024,256]{2,1,0:T(8,128)(2,1)} %get-tuple-element.16.slope_hbm), custom_call_target="tpu_custom_call" | custom-call | flops 2000000000 | bytes 16777216 | tf_op jit(solution)/shard_map/page_part/pallas_call | solution.py:340
  41.0 4.6 %all-to-all-done.1 = bf16[32,1,32,128]{3,2,1,0:T(8,128)(2,1)S(1)} async-done(((bf16[32,1,32,128]{3,2,1,0:T(8,128)(2,1)}), bf16[32,1,32,128]{3,2,1,0:T(8,128)(2,1)S(1)}, u32[]{:S(2)}, u32[]{:S(2)}) %all-to-all-start.1) | async-done | bytes 262176 | tf_op jit(solution)/shard_map/all_to_all | solution.py:337
  45.7 0.7 %convert_reduce_fusion = f32[32,128]{1,0:T(8,128)} fusion(bf16[32,1,32,128]{3,2,1,0:T(8,128)(2,1)S(1)} %all-to-all-done.1), kind=kLoop, calls=%fused_computation | loop fusion | flops 258048 | bytes 278528 | tf_op jit(solution)/shard_map/reduce_sum | solution.py:357
Async XLA Ops:
  2.1 17.8 %all-to-all-start = ((bf16[32,1,32,128]{3,2,1,0:T(8,128)(2,1)}), bf16[32,1,32,128]{3,2,1,0:T(8,128)(2,1)S(1)}, u32[]{:S(2)}, u32[]{:S(2)}) async-start(bf16[32,1,32,128]{3,2,1,0:T(8,128)(2,1)} %broadcast_in_dim.9), calls=%async_computation | async-start | bytes 524288 | tf_op jit(solution)/shard_map/all_to_all | solution.py:289
  9.4 1.9 %copy-start.2 = (s32[6,32]{1,0:T(8,128)S(1)}, s32[6,32]{1,0:T(8,128)}, u32[]{:S(2)}) copy-start(s32[6,32]{1,0:T(8,128)} %users_ref.1) | copy-start | bytes 2308
  9.4 1.9 %copy-start.3 = (f32[6,32]{1,0:T(8,128)S(1)}, f32[6,32]{1,0:T(8,128)}, u32[]{:S(2)}) copy-start(f32[6,32]{1,0:T(8,128)} %teacher_ref.1) | copy-start | bytes 2308
  9.4 1.9 %copy-start.4 = (s32[6]{0:T(128)S(1)}, s32[6]{0:T(128)}, u32[]{:S(2)}) copy-start(s32[6]{0:T(128)} %count.1) | copy-start | bytes 76
  9.4 10.4 %copy-start = (bf16[6,1024,128]{2,1,0:T(8,128)(2,1)S(1)}, bf16[6,1024,128]{2,1,0:T(8,128)(2,1)}, u32[]{:S(2)}) copy-start(bf16[6,1024,128]{2,1,0:T(8,128)(2,1)} %page_ref.1) | copy-start | bytes 4718596
  30.6 0.7 %copy-start.1 = (bf16[32,32,128]{2,1,0:T(8,128)(2,1)}, bf16[32,32,128]{2,1,0:T(8,128)(2,1)S(1)}, u32[]{:S(2)}) copy-start(bf16[32,32,128]{2,1,0:T(8,128)(2,1)S(1)} %get-tuple-element.15) | copy-start | bytes 786436
  31.3 14.3 %all-to-all-start.1 = ((bf16[32,1,32,128]{3,2,1,0:T(8,128)(2,1)}), bf16[32,1,32,128]{3,2,1,0:T(8,128)(2,1)S(1)}, u32[]{:S(2)}, u32[]{:S(2)}) async-start(bf16[32,1,32,128]{3,2,1,0:T(8,128)(2,1)} %bitcast.11), calls=%async_computation.1 | async-start | bytes 524288 | tf_op jit(solution)/shard_map/all_to_all | solution.py:337
